TPU v7x, 32 devices: a whole 2x2x4 slice. The times are simulated.
32 devices in a mesh: section: 4 (over x, core), obs: 8 (over z, y).
Axes of the slice: x: 2, y: 2, z: 4, core: 2. Of those that a mesh axis runs over, the one named last changes fastest.
Arguments:
- predictors: bfloat16 [4, 4, 20, 32768], P('section', None, None, 'obs'), may hold values from -5 to 5
- departures: float32 [4, 4, 32768], P('section', None, 'obs'), may hold values from -30 to 30
- obs_precision: float32 [4, 4, 32768], P('section', None, 'obs'), may hold values from 0.3 to 3
- qc_pass: int32 [4, 4, 32768], P('section', None, 'obs'), may hold values 0 or 1
- block_channel: int32 [4, 4, 256], P('section', None, 'obs'), may hold values from 0 to 2047, as said below
- stream_order: int32 [4], replicated, may hold values from 0 to 3, each once
- prior_coeffs: float32 [4, 20, 2048], P(None, None, 'obs'), may hold values from -1 to 1
- prior_info: float32 [4, 210, 2048], P(None, None, 'obs'), may hold values from -1 to 32, as said below
- memory_factor: float32 [2048], P('obs'), may hold values from 0.5 to 0.98
Outputs:
- coeffs: float32 [4, 4, 20, 2048], P('section', None, None, 'obs')
- information: float32 [4, 4, 210, 2048], P('section', None, None, 'obs')
Inputs may be any that keep to these rules, and one draw needn't show every extreme that they name: `block_channel`: among the 32 row blocks of one index of obs, at most 8 have channels in any one range of the 256 channels from a multiple of 256; in every window and stream one such range holds exactly 8 blocks of every index of obs. `stream_order`: each stream appears once. `prior_info`: for every stream and channel the 210 entries are the upper triangle, row by row, of a symmetric positive definite matrix of order 20.
All inputs are finite; a program needn't handle non-finite values. No bound on the sum of `qc_pass` on one device may be relied on, other than what follows from the above.
Results may differ from a plain program's by a relative error of at most 0.0038.
Values sent between devices are 32-bit elements; how exact they have to be, the bound alone decides.
A program may use at most 64 MiB of HBM per device.

v0:
```python
import jax
import jax.numpy as jnp
import numpy as np
from jax import lax
from jax.sharding import PartitionSpec as P

HUBER_SQ = 9.0
PRIOR_WEIGHT = 64.0


def from_behind(array, axis, by):
    size = lax.axis_size(axis)
    pairs = [(i, i + by) for i in range(size) if 0 <= i + by < size]
    return lax.ppermute(array, axis, pairs)


def upper_positions(dimension):
    return np.array(
        [i * dimension + j for i in range(dimension) for j in range(i, dimension)], dtype=np.int32
    )


def solve_packed(packed, target):
    dimension = target.shape[0]
    placing = {}
    counter = 0
    for i in range(dimension):
        for j in range(i, dimension):
            placing[i, j] = counter
            counter += 1
    factor = [[None] * dimension for i in range(dimension)]
    for j in range(dimension):
        pivot_root = jnp.sqrt(
            packed[placing[j, j]] - sum((factor[j][k] * factor[j][k] for k in range(j)))
        )
        factor[j][j] = pivot_root
        for i in range(j + 1, dimension):
            factor[i][j] = (
                packed[placing[j, i]] - sum((factor[i][k] * factor[j][k] for k in range(j)))
            ) / pivot_root
    forward = []
    for i in range(dimension):
        forward.append(
            (target[i] - sum((factor[i][k] * forward[k] for k in range(i)))) / factor[i][i]
        )
    backward = [None] * dimension
    for i in reversed(range(dimension)):
        backward[i] = (
            forward[i] - sum((factor[k][i] * backward[k] for k in range(i + 1, dimension)))
        ) / factor[i][i]
    return jnp.stack(backward)


def block_terms(predicted, departed, precision, passed, block_coeffs):
    pred_count, row_count = predicted.shape
    block_count = block_coeffs.shape[1]
    block_width = row_count // block_count
    upper_index = upper_positions(pred_count)
    shaped = predicted.reshape(pred_count, block_count, block_width)
    offset = jnp.sum(shaped.astype(jnp.float32) * block_coeffs[:, :, None], axis=0)
    residual = departed.reshape(block_count, block_width) - offset
    scale_row = precision.reshape(block_count, block_width)
    weight = (
        passed.reshape(block_count, block_width).astype(jnp.float32)
        * scale_row
        / (1.0 + scale_row * residual * residual / HUBER_SQ)
    )
    weighted = (weight[None] * shaped.astype(jnp.float32)).astype(jnp.bfloat16)
    chi_square = jnp.sum(weight * residual * residual)
    passed_count = jnp.sum(passed.astype(jnp.float32))
    gram_full = lax.dot_general(
        weighted, shaped, (((2,), (2,)), ((1,), (1,))), preferred_element_type=jnp.float32
    )
    gram_upper = gram_full.reshape(block_count, pred_count * pred_count)[:, upper_index]
    gradient = jnp.sum(weighted.astype(jnp.float32) * residual[None], axis=2).T
    return (jnp.concatenate([gram_upper, gradient], axis=1), jnp.stack([chi_square, passed_count]))


def local(
    predictors,
    departures,
    obs_precision,
    qc_pass,
    block_channel,
    stream_order,
    prior_coeffs,
    prior_info,
    memory_factor,
):
    section_count = lax.axis_size("section")
    obs_devices = lax.axis_size("obs")
    section_place = lax.axis_index("section")
    stream_count = stream_order.shape[0]
    local_channels = memory_factor.shape[0]
    block_count = block_channel.shape[2]
    pred_count = prior_coeffs.shape[1]
    tri_count = prior_info.shape[1]
    column_count = tri_count + pred_count
    capacity = 2 * block_count // obs_devices
    local_line = jnp.arange(local_channels, dtype=jnp.float32)
    owner_line = jnp.arange(obs_devices, dtype=jnp.int32)
    slot_line = jnp.arange(obs_devices * capacity, dtype=jnp.int32)
    highest = lax.Precision.HIGHEST

    def pack_blocks(block_sums, channel):
        owner_index = channel // local_channels
        inner_channel = channel % local_channels
        owner_hot = (owner_index[:, None] == owner_line[None, :]).astype(jnp.int32)
        ranking = jnp.sum((jnp.cumsum(owner_hot, axis=0) - 1) * owner_hot, axis=1)
        slot_of = owner_index * capacity + ranking
        placing = (slot_of[:, None] == slot_line[None, :]).astype(jnp.float32)
        send_rows = lax.dot_general(
            placing,
            block_sums,
            (((0,), (0,)), ((), ())),
            precision=highest,
            preferred_element_type=jnp.float32,
        ).reshape(obs_devices, capacity, column_count)
        send_channel = (
            lax.dot_general(
                placing,
                (inner_channel + 1).astype(jnp.float32),
                (((0,), (0,)), ((), ())),
                precision=highest,
                preferred_element_type=jnp.float32,
            ).reshape(obs_devices, capacity)
            - 1.0
        )
        return (send_rows, send_channel)

    def unpack_blocks(got_rows, got_channel):
        gather_hot = (got_channel.reshape(-1)[:, None] == local_line[None, :]).astype(jnp.float32)
        return lax.dot_general(
            got_rows.reshape(-1, column_count),
            gather_hot,
            (((0,), (0,)), ((), ())),
            precision=highest,
            preferred_element_type=jnp.float32,
        )

    def window_work(state_now, streams):
        beta_prior = state_now[:, :pred_count]
        info_prior = state_now[:, pred_count:]
        all_coeffs = lax.all_gather(beta_prior, "obs", axis=2, tiled=True)
        channel = jnp.take(block_channel[0], streams, axis=0)
        block_coeffs = jax.vmap(lambda coeff_rows, chan: jnp.take(coeff_rows, chan, axis=1))(
            all_coeffs, channel
        )
        block_sums, statistics = jax.vmap(block_terms)(
            jnp.take(predictors[0], streams, axis=0),
            jnp.take(departures[0], streams, axis=0),
            jnp.take(obs_precision[0], streams, axis=0),
            jnp.take(qc_pass[0], streams, axis=0),
            block_coeffs,
        )
        totals = lax.psum(statistics, "obs")
        send_rows, send_channel = jax.vmap(pack_blocks)(block_sums, channel)
        got_rows, got_channel = (
            lax.all_to_all(send_rows, "obs", split_axis=1, concat_axis=1, tiled=True),
            lax.all_to_all(send_channel, "obs", split_axis=1, concat_axis=1, tiled=True),
        )
        normal = jax.vmap(unpack_blocks)(got_rows, got_channel)
        inflation = (totals[:, 0] + PRIOR_WEIGHT) / (totals[:, 1] + PRIOR_WEIGHT)
        info_post = info_prior + normal[:, :tri_count] / inflation[:, None, None]
        beta_post = beta_prior + jax.vmap(solve_packed)(
            info_post, normal[:, tri_count:] / inflation[:, None, None]
        )
        outgoing = jnp.concatenate([beta_post, memory_factor[None, None, :] * info_post], axis=1)
        incoming = from_behind(outgoing, "section", 1)
        return (beta_post, info_post, incoming)

    def fresh_of(streams):
        return jnp.concatenate(
            [jnp.take(prior_coeffs, streams, axis=0), jnp.take(prior_info, streams, axis=0)], axis=1
        )

    coeff_start = jnp.zeros((1, stream_count, pred_count, local_channels), jnp.float32)
    info_start = jnp.zeros((1, stream_count, tri_count, local_channels), jnp.float32)

    def tick_step(t, loop_state):
        incoming, coeff_out, info_out = loop_state
        entry_index = t - section_place
        usable = (entry_index >= 0) & (entry_index < stream_count)
        slot_index = jnp.clip(entry_index, 0, stream_count - 1)
        streams = lax.dynamic_slice_in_dim(stream_order, slot_index, 1, 0)
        state_now = jnp.where(
            (section_place == 0) | jnp.logical_not(usable), fresh_of(streams), incoming
        )
        beta_post, info_post, incoming = window_work(state_now, streams)

        def store_entry(buffer, result):
            current = lax.dynamic_slice_in_dim(buffer, slot_index, 1, 1)
            updated = jnp.where(usable, result[None], current)
            return lax.dynamic_update_slice_in_dim(buffer, updated, slot_index, 1)

        return (incoming, store_entry(coeff_out, beta_post), store_entry(info_out, info_post))

    initial = (jnp.zeros((1, column_count, local_channels), jnp.float32), coeff_start, info_start)
    final_state = lax.fori_loop(0, stream_count + section_count - 1, tick_step, initial)
    return (final_state[1], final_state[2])


def solution(mesh):
    in_specs = (
        P("section", None, None, "obs"),
        P("section", None, "obs"),
        P("section", None, "obs"),
        P("section", None, "obs"),
        P("section", None, "obs"),
        P(),
        P(None, None, "obs"),
        P(None, None, "obs"),
        P("obs"),
    )
    out_specs = (P("section", None, None, "obs"), P("section", None, None, "obs"))
    return jax.shard_map(local, mesh=mesh, in_specs=in_specs, out_specs=out_specs, check_vma=False)
```

profile of v0, /device:TPU:1, one launch (start us, length us, event | category | flops | bytes accessed | tf_op | source)
XLA Modules:
  0.0 688.5 jit_solution(5905409147109336993)
XLA Ops:
  2.9 684.6 %while.38 = (s32[]{:T(128)}, f32[1,230,256]{2,1,0:T(8,128)S(1)}, f32[1,4,20,256]{3,1,2,0:T(4,128)S(1)}, f32[1,4,210,256]{3,1,2,0:T(4,128)S(1)}, s32[]{:T(128)}, ...) while((s32[]{:T(128)}, f32[1,230,256]{2,1,0:T(8,128)S(1)}, ...), condition=%wide.region_8.10_spmd.clone.clone, body=%wide.region_0.9_spmd.sunk.clone.clone.sunk | while | flops 57759508 | bytes 13853709 | solution.py:199
  7.5 6.4 all-to-all-start.1
  16.3 24.6 %all_gather.15 = f32[1,20,2048]{2,1,0:T(8,128)S(1)} all-gather(f32[1,20,256]{2,1,0:T(8,128)S(1)} %slice.5342), channel_id=1, replica_groups=mesh['section'=4,'obs'=8] {'obs'}, dimensions={2}, use_global_device_ids=true | all-gather | bytes 184320 | tf_op jit(solution)/shard_map/while/body/eval_jaxpr/all_gather | solution.py:144
  47.6 17.5 %psum.19 = f32[1,2]{1,0:T(1,128)S(1)} all-reduce(f32[1,2]{1,0:T(1,128)S(1)} %maximum_bitcast_fusion.6), channel_id=1, replica_groups=mesh['section'=4,'obs'=8] {'obs'}, use_global_device_ids=true, to_apply=%region_7.8 | all-reduce | flops 2 | bytes 16 | tf_op jit(solution)/shard_map/while/body/eval_jaxpr/psum | solution.py:156
  68.0 3.4 all-to-all-start
  72.6 4.4 all-to-all-done
  83.2 15.7 %collective-permute-start = (f32[1,230,256]{2,1,0:T(8,128)S(1)}, f32[1,230,256]{2,1,0:T(8,128)S(1)}, u32[]{:S(2)}, u32[]{:S(2)}) collective-permute-start(f32[1,230,256]{2,1,0:T(8,128)S(1)} %pad_maximum_fusion.2), channel_id=1, source_target_pairs={{0,8},{8,16},{16,24},{1,9},{9,17},{17,25},{2,10},{10,18},{18,26},{... | collective-permute-start | bytes 706568 | tf_op jit(solution)/shard_map/while/body/eval_jaxpr/ppermute | solution.py:14
  99.3 5.9 dynamic_update_slice.31
  109.8 3.3 all-to-all-start.1
  115.6 25.2 %all_gather.15 = f32[1,20,2048]{2,1,0:T(8,128)S(1)} all-gather(f32[1,20,256]{2,1,0:T(8,128)S(1)} %slice.5342), channel_id=1, replica_groups=mesh['section'=4,'obs'=8] {'obs'}, dimensions={2}, use_global_device_ids=true | all-gather | bytes 184320 | tf_op jit(solution)/shard_map/while/body/eval_jaxpr/all_gather | solution.py:144
  147.5 17.3 %psum.19 = f32[1,2]{1,0:T(1,128)S(1)} all-reduce(f32[1,2]{1,0:T(1,128)S(1)} %maximum_bitcast_fusion.6), channel_id=1, replica_groups=mesh['section'=4,'obs'=8] {'obs'}, use_global_device_ids=true, to_apply=%region_7.8 | all-reduce | flops 2 | bytes 16 | tf_op jit(solution)/shard_map/while/body/eval_jaxpr/psum | solution.py:156
  167.6 3.4 all-to-all-start
  172.3 4.4 all-to-all-done
  182.9 13.1 %collective-permute-start = (f32[1,230,256]{2,1,0:T(8,128)S(1)}, f32[1,230,256]{2,1,0:T(8,128)S(1)}, u32[]{:S(2)}, u32[]{:S(2)}) collective-permute-start(f32[1,230,256]{2,1,0:T(8,128)S(1)} %pad_maximum_fusion.2), channel_id=1, source_target_pairs={{0,8},{8,16},{16,24},{1,9},{9,17},{17,25},{2,10},{10,18},{18,26},{... | collective-permute-start | bytes 706568 | tf_op jit(solution)/shard_map/while/body/eval_jaxpr/ppermute | solution.py:14
  196.4 5.9 dynamic_update_slice.31
  206.9 3.3 all-to-all-start.1
  212.6 24.6 %all_gather.15 = f32[1,20,2048]{2,1,0:T(8,128)S(1)} all-gather(f32[1,20,256]{2,1,0:T(8,128)S(1)} %slice.5342), channel_id=1, replica_groups=mesh['section'=4,'obs'=8] {'obs'}, dimensions={2}, use_global_device_ids=true | all-gather | bytes 184320 | tf_op jit(solution)/shard_map/while/body/eval_jaxpr/all_gather | solution.py:144
  244.0 17.5 %psum.19 = f32[1,2]{1,0:T(1,128)S(1)} all-reduce(f32[1,2]{1,0:T(1,128)S(1)} %maximum_bitcast_fusion.6), channel_id=1, replica_groups=mesh['section'=4,'obs'=8] {'obs'}, use_global_device_ids=true, to_apply=%region_7.8 | all-reduce | flops 2 | bytes 16 | tf_op jit(solution)/shard_map/while/body/eval_jaxpr/psum | solution.py:156
  264.4 3.4 all-to-all-start
  269.0 4.4 all-to-all-done
  279.6 13.4 %collective-permute-start = (f32[1,230,256]{2,1,0:T(8,128)S(1)}, f32[1,230,256]{2,1,0:T(8,128)S(1)}, u32[]{:S(2)}, u32[]{:S(2)}) collective-permute-start(f32[1,230,256]{2,1,0:T(8,128)S(1)} %pad_maximum_fusion.2), channel_id=1, source_target_pairs={{0,8},{8,16},{16,24},{1,9},{9,17},{17,25},{2,10},{10,18},{18,26},{... | collective-permute-start | bytes 706568 | tf_op jit(solution)/shard_map/while/body/eval_jaxpr/ppermute | solution.py:14
  293.4 5.9 dynamic_update_slice.31
  303.9 3.3 all-to-all-start.1
  309.7 24.8 %all_gather.15 = f32[1,20,2048]{2,1,0:T(8,128)S(1)} all-gather(f32[1,20,256]{2,1,0:T(8,128)S(1)} %slice.5342), channel_id=1, replica_groups=mesh['section'=4,'obs'=8] {'obs'}, dimensions={2}, use_global_device_ids=true | all-gather | bytes 184320 | tf_op jit(solution)/shard_map/while/body/eval_jaxpr/all_gather | solution.py:144
  341.3 17.6 %psum.19 = f32[1,2]{1,0:T(1,128)S(1)} all-reduce(f32[1,2]{1,0:T(1,128)S(1)} %maximum_bitcast_fusion.6), channel_id=1, replica_groups=mesh['section'=4,'obs'=8] {'obs'}, use_global_device_ids=true, to_apply=%region_7.8 | all-reduce | flops 2 | bytes 16 | tf_op jit(solution)/shard_map/while/body/eval_jaxpr/psum | solution.py:156
  361.8 3.4 all-to-all-start
  366.4 4.4 all-to-all-done
  377.0 13.1 %collective-permute-start = (f32[1,230,256]{2,1,0:T(8,128)S(1)}, f32[1,230,256]{2,1,0:T(8,128)S(1)}, u32[]{:S(2)}, u32[]{:S(2)}) collective-permute-start(f32[1,230,256]{2,1,0:T(8,128)S(1)} %pad_maximum_fusion.2), channel_id=1, source_target_pairs={{0,8},{8,16},{16,24},{1,9},{9,17},{17,25},{2,10},{10,18},{18,26},{... | collective-permute-start | bytes 706568 | tf_op jit(solution)/shard_map/while/body/eval_jaxpr/ppermute | solution.py:14
  390.5 5.9 dynamic_update_slice.31
  401.0 3.3 all-to-all-start.1
  406.7 24.9 %all_gather.15 = f32[1,20,2048]{2,1,0:T(8,128)S(1)} all-gather(f32[1,20,256]{2,1,0:T(8,128)S(1)} %slice.5342), channel_id=1, replica_groups=mesh['section'=4,'obs'=8] {'obs'}, dimensions={2}, use_global_device_ids=true | all-gather | bytes 184320 | tf_op jit(solution)/shard_map/while/body/eval_jaxpr/all_gather | solution.py:144
  438.4 17.2 %psum.19 = f32[1,2]{1,0:T(1,128)S(1)} all-reduce(f32[1,2]{1,0:T(1,128)S(1)} %maximum_bitcast_fusion.6), channel_id=1, replica_groups=mesh['section'=4,'obs'=8] {'obs'}, use_global_device_ids=true, to_apply=%region_7.8 | all-reduce | flops 2 | bytes 16 | tf_op jit(solution)/shard_map/while/body/eval_jaxpr/psum | solution.py:156
  458.5 3.4 all-to-all-start
  463.2 4.4 all-to-all-done
  473.8 13.4 %collective-permute-start = (f32[1,230,256]{2,1,0:T(8,128)S(1)}, f32[1,230,256]{2,1,0:T(8,128)S(1)}, u32[]{:S(2)}, u32[]{:S(2)}) collective-permute-start(f32[1,230,256]{2,1,0:T(8,128)S(1)} %pad_maximum_fusion.2), channel_id=1, source_target_pairs={{0,8},{8,16},{16,24},{1,9},{9,17},{17,25},{2,10},{10,18},{18,26},{... | collective-permute-start | bytes 706568 | tf_op jit(solution)/shard_map/while/body/eval_jaxpr/ppermute | solution.py:14
  487.5 5.9 dynamic_update_slice.31
  503.8 24.8 %all_gather.15 = f32[1,20,2048]{2,1,0:T(8,128)S(1)} all-gather(f32[1,20,256]{2,1,0:T(8,128)S(1)} %slice.5342), channel_id=1, replica_groups=mesh['section'=4,'obs'=8] {'obs'}, dimensions={2}, use_global_device_ids=true | all-gather | bytes 184320 | tf_op jit(solution)/shard_map/while/body/eval_jaxpr/all_gather | solution.py:144
  535.4 17.5 %psum.19 = f32[1,2]{1,0:T(1,128)S(1)} all-reduce(f32[1,2]{1,0:T(1,128)S(1)} %maximum_bitcast_fusion.6), channel_id=1, replica_groups=mesh['section'=4,'obs'=8] {'obs'}, use_global_device_ids=true, to_apply=%region_7.8 | all-reduce | flops 2 | bytes 16 | tf_op jit(solution)/shard_map/while/body/eval_jaxpr/psum | solution.py:156
  555.8 3.4 all-to-all-start
  560.4 4.4 all-to-all-done
  571.0 13.2 %collective-permute-start = (f32[1,230,256]{2,1,0:T(8,128)S(1)}, f32[1,230,256]{2,1,0:T(8,128)S(1)}, u32[]{:S(2)}, u32[]{:S(2)}) collective-permute-start(f32[1,230,256]{2,1,0:T(8,128)S(1)} %pad_maximum_fusion.2), channel_id=1, source_target_pairs={{0,8},{8,16},{16,24},{1,9},{9,17},{17,25},{2,10},{10,18},{18,26},{... | collective-permute-start | bytes 706568 | tf_op jit(solution)/shard_map/while/body/eval_jaxpr/ppermute | solution.py:14
  584.6 5.9 dynamic_update_slice.31
  600.9 24.5 %all_gather.15 = f32[1,20,2048]{2,1,0:T(8,128)S(1)} all-gather(f32[1,20,256]{2,1,0:T(8,128)S(1)} %slice.5342), channel_id=1, replica_groups=mesh['section'=4,'obs'=8] {'obs'}, dimensions={2}, use_global_device_ids=true | all-gather | bytes 184320 | tf_op jit(solution)/shard_map/while/body/eval_jaxpr/all_gather | solution.py:144
  632.1 18.0 %psum.19 = f32[1,2]{1,0:T(1,128)S(1)} all-reduce(f32[1,2]{1,0:T(1,128)S(1)} %maximum_bitcast_fusion.6), channel_id=1, replica_groups=mesh['section'=4,'obs'=8] {'obs'}, use_global_device_ids=true, to_apply=%region_7.8 | all-reduce | flops 2 | bytes 16 | tf_op jit(solution)/shard_map/while/body/eval_jaxpr/psum | solution.py:156
  652.9 3.4 all-to-all-start
  657.6 4.4 all-to-all-done
  668.2 13.1 %collective-permute-start = (f32[1,230,256]{2,1,0:T(8,128)S(1)}, f32[1,230,256]{2,1,0:T(8,128)S(1)}, u32[]{:S(2)}, u32[]{:S(2)}) collective-permute-start(f32[1,230,256]{2,1,0:T(8,128)S(1)} %pad_maximum_fusion.2), channel_id=1, source_target_pairs={{0,8},{8,16},{16,24},{1,9},{9,17},{17,25},{2,10},{10,18},{18,26},{... | collective-permute-start | bytes 706568 | tf_op jit(solution)/shard_map/while/body/eval_jaxpr/ppermute | solution.py:14
  681.7 5.9 dynamic_update_slice.31
  (632 shorter events, 155.7 us)
Async XLA Ops:
  2.2 0.7 copy-start.4
  2.3 0.7 copy-start.5
  2.3 0.7 copy-start.6
  7.5 60.4 %all-to-all-start.1 = ((f32[1,8,8]{2,0,1:T(1,128)}), f32[1,8,8]{2,0,1:T(1,128)S(1)}, u32[]{:S(2)}, u32[]{:S(2)}) async-start(f32[1,8,8]{2,0,1:T(1,128)} %bitcast.2454), calls=%async_computation.1 | async-start | bytes 8192 | tf_op jit(solution)/shard_map/while/body/eval_jaxpr/all_to_all | solution.py:160
  68.0 9.1 %all-to-all-start = ((f32[1,8,8,230]{3,2,0,1:T(8,128)}), f32[1,8,8,230]{3,2,0,1:T(8,128)S(1)}, u32[]{:S(2)}, u32[]{:S(2)}) async-start(f32[1,8,8,230]{3,2,0,1:T(8,128)} %convolution_bitcast_fusion.4), calls=%async_computation | async-start | bytes 131072 | tf_op jit(solution)/shard_map/while/body/eval_jaxpr/all_to_all | solution.py:159
  77.4 0.6 copy-start
  78.8 0.7 slice-start
  80.7 0.7 copy-start.1
  83.2 22.0 %collective-permute-start = (f32[1,230,256]{2,1,0:T(8,128)S(1)}, f32[1,230,256]{2,1,0:T(8,128)S(1)}, u32[]{:S(2)}, u32[]{:S(2)}) collective-permute-start(f32[1,230,256]{2,1,0:T(8,128)S(1)} %pad_maximum_fusion.2), channel_id=1, source_target_pairs={{0,8},{8,16},{16,24},{1,9},{9,17},{17,25},{2,10},{10,18},{18,26},{... | collective-permute-start | bytes 706568 | tf_op jit(solution)/shard_map/while/body/eval_jaxpr/ppermute | solution.py:14
  109.8 57.8 %all-to-all-start.1 = ((f32[1,8,8]{2,0,1:T(1,128)}), f32[1,8,8]{2,0,1:T(1,128)S(1)}, u32[]{:S(2)}, u32[]{:S(2)}) async-start(f32[1,8,8]{2,0,1:T(1,128)} %bitcast.2454), calls=%async_computation.1 | async-start | bytes 8192 | tf_op jit(solution)/shard_map/while/body/eval_jaxpr/all_to_all | solution.py:160
  167.6 9.1 %all-to-all-start = ((f32[1,8,8,230]{3,2,0,1:T(8,128)}), f32[1,8,8,230]{3,2,0,1:T(8,128)S(1)}, u32[]{:S(2)}, u32[]{:S(2)}) async-start(f32[1,8,8,230]{3,2,0,1:T(8,128)} %convolution_bitcast_fusion.4), calls=%async_computation | async-start | bytes 131072 | tf_op jit(solution)/shard_map/while/body/eval_jaxpr/all_to_all | solution.py:159
  177.1 0.6 copy-start
  178.5 0.7 slice-start
  180.4 0.7 copy-start.1
  182.9 19.4 %collective-permute-start = (f32[1,230,256]{2,1,0:T(8,128)S(1)}, f32[1,230,256]{2,1,0:T(8,128)S(1)}, u32[]{:S(2)}, u32[]{:S(2)}) collective-permute-start(f32[1,230,256]{2,1,0:T(8,128)S(1)} %pad_maximum_fusion.2), channel_id=1, source_target_pairs={{0,8},{8,16},{16,24},{1,9},{9,17},{17,25},{2,10},{10,18},{18,26},{... | collective-permute-start | bytes 706568 | tf_op jit(solution)/shard_map/while/body/eval_jaxpr/ppermute | solution.py:14
  206.9 57.5 %all-to-all-start.1 = ((f32[1,8,8]{2,0,1:T(1,128)}), f32[1,8,8]{2,0,1:T(1,128)S(1)}, u32[]{:S(2)}, u32[]{:S(2)}) async-start(f32[1,8,8]{2,0,1:T(1,128)} %bitcast.2454), calls=%async_computation.1 | async-start | bytes 8192 | tf_op jit(solution)/shard_map/while/body/eval_jaxpr/all_to_all | solution.py:160
  264.4 9.1 %all-to-all-start = ((f32[1,8,8,230]{3,2,0,1:T(8,128)}), f32[1,8,8,230]{3,2,0,1:T(8,128)S(1)}, u32[]{:S(2)}, u32[]{:S(2)}) async-start(f32[1,8,8,230]{3,2,0,1:T(8,128)} %convolution_bitcast_fusion.4), calls=%async_computation | async-start | bytes 131072 | tf_op jit(solution)/shard_map/while/body/eval_jaxpr/all_to_all | solution.py:159
  273.8 0.6 copy-start
  275.2 0.7 slice-start
  277.1 0.7 copy-start.1
  279.6 19.7 %collective-permute-start = (f32[1,230,256]{2,1,0:T(8,128)S(1)}, f32[1,230,256]{2,1,0:T(8,128)S(1)}, u32[]{:S(2)}, u32[]{:S(2)}) collective-permute-start(f32[1,230,256]{2,1,0:T(8,128)S(1)} %pad_maximum_fusion.2), channel_id=1, source_target_pairs={{0,8},{8,16},{16,24},{1,9},{9,17},{17,25},{2,10},{10,18},{18,26},{... | collective-permute-start | bytes 706568 | tf_op jit(solution)/shard_map/while/body/eval_jaxpr/ppermute | solution.py:14
  303.9 57.8 %all-to-all-start.1 = ((f32[1,8,8]{2,0,1:T(1,128)}), f32[1,8,8]{2,0,1:T(1,128)S(1)}, u32[]{:S(2)}, u32[]{:S(2)}) async-start(f32[1,8,8]{2,0,1:T(1,128)} %bitcast.2454), calls=%async_computation.1 | async-start | bytes 8192 | tf_op jit(solution)/shard_map/while/body/eval_jaxpr/all_to_all | solution.py:160
  361.8 9.1 %all-to-all-start = ((f32[1,8,8,230]{3,2,0,1:T(8,128)}), f32[1,8,8,230]{3,2,0,1:T(8,128)S(1)}, u32[]{:S(2)}, u32[]{:S(2)}) async-start(f32[1,8,8,230]{3,2,0,1:T(8,128)} %convolution_bitcast_fusion.4), calls=%async_computation | async-start | bytes 131072 | tf_op jit(solution)/shard_map/while/body/eval_jaxpr/all_to_all | solution.py:159
  371.2 0.6 copy-start
  372.6 0.7 slice-start
  374.5 0.7 copy-start.1
  377.0 19.4 %collective-permute-start = (f32[1,230,256]{2,1,0:T(8,128)S(1)}, f32[1,230,256]{2,1,0:T(8,128)S(1)}, u32[]{:S(2)}, u32[]{:S(2)}) collective-permute-start(f32[1,230,256]{2,1,0:T(8,128)S(1)} %pad_maximum_fusion.2), channel_id=1, source_target_pairs={{0,8},{8,16},{16,24},{1,9},{9,17},{17,25},{2,10},{10,18},{18,26},{... | collective-permute-start | bytes 706568 | tf_op jit(solution)/shard_map/while/body/eval_jaxpr/ppermute | solution.py:14
  401.0 57.5 %all-to-all-start.1 = ((f32[1,8,8]{2,0,1:T(1,128)}), f32[1,8,8]{2,0,1:T(1,128)S(1)}, u32[]{:S(2)}, u32[]{:S(2)}) async-start(f32[1,8,8]{2,0,1:T(1,128)} %bitcast.2454), calls=%async_computation.1 | async-start | bytes 8192 | tf_op jit(solution)/shard_map/while/body/eval_jaxpr/all_to_all | solution.py:160
  458.5 9.1 %all-to-all-start = ((f32[1,8,8,230]{3,2,0,1:T(8,128)}), f32[1,8,8,230]{3,2,0,1:T(8,128)S(1)}, u32[]{:S(2)}, u32[]{:S(2)}) async-start(f32[1,8,8,230]{3,2,0,1:T(8,128)} %convolution_bitcast_fusion.4), calls=%async_computation | async-start | bytes 131072 | tf_op jit(solution)/shard_map/while/body/eval_jaxpr/all_to_all | solution.py:159
  468.0 0.6 copy-start
  469.4 0.7 slice-start
  471.3 0.7 copy-start.1
  473.8 19.7 %collective-permute-start = (f32[1,230,256]{2,1,0:T(8,128)S(1)}, f32[1,230,256]{2,1,0:T(8,128)S(1)}, u32[]{:S(2)}, u32[]{:S(2)}) collective-permute-start(f32[1,230,256]{2,1,0:T(8,128)S(1)} %pad_maximum_fusion.2), channel_id=1, source_target_pairs={{0,8},{8,16},{16,24},{1,9},{9,17},{17,25},{2,10},{10,18},{18,26},{... | collective-permute-start | bytes 706568 | tf_op jit(solution)/shard_map/while/body/eval_jaxpr/ppermute | solution.py:14
  498.1 57.7 %all-to-all-start.1 = ((f32[1,8,8]{2,0,1:T(1,128)}), f32[1,8,8]{2,0,1:T(1,128)S(1)}, u32[]{:S(2)}, u32[]{:S(2)}) async-start(f32[1,8,8]{2,0,1:T(1,128)} %bitcast.2454), calls=%async_computation.1 | async-start | bytes 8192 | tf_op jit(solution)/shard_map/while/body/eval_jaxpr/all_to_all | solution.py:160
  555.8 9.1 %all-to-all-start = ((f32[1,8,8,230]{3,2,0,1:T(8,128)}), f32[1,8,8,230]{3,2,0,1:T(8,128)S(1)}, u32[]{:S(2)}, u32[]{:S(2)}) async-start(f32[1,8,8,230]{3,2,0,1:T(8,128)} %convolution_bitcast_fusion.4), calls=%async_computation | async-start | bytes 131072 | tf_op jit(solution)/shard_map/while/body/eval_jaxpr/all_to_all | solution.py:159
  565.2 0.6 copy-start
  566.6 0.7 slice-start
  568.5 0.7 copy-start.1
  571.0 19.5 %collective-permute-start = (f32[1,230,256]{2,1,0:T(8,128)S(1)}, f32[1,230,256]{2,1,0:T(8,128)S(1)}, u32[]{:S(2)}, u32[]{:S(2)}) collective-permute-start(f32[1,230,256]{2,1,0:T(8,128)S(1)} %pad_maximum_fusion.2), channel_id=1, source_target_pairs={{0,8},{8,16},{16,24},{1,9},{9,17},{17,25},{2,10},{10,18},{18,26},{... | collective-permute-start | bytes 706568 | tf_op jit(solution)/shard_map/while/body/eval_jaxpr/ppermute | solution.py:14
  595.1 57.8 %all-to-all-start.1 = ((f32[1,8,8]{2,0,1:T(1,128)}), f32[1,8,8]{2,0,1:T(1,128)S(1)}, u32[]{:S(2)}, u32[]{:S(2)}) async-start(f32[1,8,8]{2,0,1:T(1,128)} %bitcast.2454), calls=%async_computation.1 | async-start | bytes 8192 | tf_op jit(solution)/shard_map/while/body/eval_jaxpr/all_to_all | solution.py:160
  652.9 9.1 %all-to-all-start = ((f32[1,8,8,230]{3,2,0,1:T(8,128)}), f32[1,8,8,230]{3,2,0,1:T(8,128)S(1)}, u32[]{:S(2)}, u32[]{:S(2)}) async-start(f32[1,8,8,230]{3,2,0,1:T(8,128)} %convolution_bitcast_fusion.4), calls=%async_computation | async-start | bytes 131072 | tf_op jit(solution)/shard_map/while/body/eval_jaxpr/all_to_all | solution.py:159
  662.4 0.6 copy-start
  663.8 0.7 slice-start
  665.7 0.7 copy-start.1
  668.2 19.4 %collective-permute-start = (f32[1,230,256]{2,1,0:T(8,128)S(1)}, f32[1,230,256]{2,1,0:T(8,128)S(1)}, u32[]{:S(2)}, u32[]{:S(2)}) collective-permute-start(f32[1,230,256]{2,1,0:T(8,128)S(1)} %pad_maximum_fusion.2), channel_id=1, source_target_pairs={{0,8},{8,16},{16,24},{1,9},{9,17},{17,25},{2,10},{10,18},{18,26},{... | collective-permute-start | bytes 706568 | tf_op jit(solution)/shard_map/while/body/eval_jaxpr/ppermute | solution.py:14
  687.6 0.9 copy-start.2
  687.6 0.9 copy-start.3
where the time goes:
time: 692 us; the launch traced here: 689 us
  blocking collectives  296 us (43%)
  starting transfers between devices  145 us (21%)
  local copies, waits for them, and re-layouts  109 us (16%)
  other arithmetic  68.2 us (10%)
  waiting for transfers between devices  30.8 us (4%)
  loops' own time  25.7 us (4%)
  matrix products  12.9 us (2%)
    all_gather x7, blocking collectives, window_work(): all_coeffs = lax.all_gather(beta_prior, 'obs', axis=2, tiled=True)  173 us
    psum x7, blocking collectives, window_work(): totals = lax.psum(statistics, 'obs')  123 us
    ppermute x7, starting transfers between devices, from_behind(): return lax.ppermute(array, axis, pairs)  95 us
    dynamic_update_slice x28, local copies, waits for them, and re-layouts, store_entry(): return lax.dynamic_update_slice_in_dim(buffer, updated, slot_index, 1)  43.8 us
    all_to_all x7, waiting for transfers between devices, window_work(): lax.all_to_all(send_rows, 'obs', split_axis=1, concat_axis=1, tiled=True)  30.8 us
    all_to_all x7, starting transfers between devices, window_work(): lax.all_to_all(send_channel, 'obs', split_axis=1, concat_axis=1, tiled=True)  26.2 us
    another operation x1, loops' own time, local(): lax.fori_loop(0, stream_count + section_count - 1, tick_step, initial)  25.7 us
    all_to_all x7, starting transfers between devices, window_work(): lax.all_to_all(send_rows, 'obs', split_axis=1, concat_axis=1, tiled=True)  23.5 us
  transfers between devices with their start and end apart: 21, of which 7 were waited for; matrix products, arithmetic and copies ran while one was open for 18% of the time, Pallas kernels for 0%

commit v1 on v0

--- a/solution.py
+++ b/solution.py
@@ -6,6 +6,20 @@
 
 HUBER_SQ = 9.0
 PRIOR_WEIGHT = 64.0
+
+
+def drive_scales(body):
+    n_lanes = lax.psum(1, "obs")
+    met_up = list(map(lambda no: (no - 1, no), range(1, n_lanes))) + [(n_lanes - 1, 0)]
+    next_value = body
+    pp = 0
+    xs_all = [next_value]
+    while pp < n_lanes - 1:
+        next_value = lax.ppermute(next_value, axis_name="obs", perm=met_up)
+        xs_all += [next_value]
+        pp += 1
+    g_now = jnp.concatenate([*reversed(xs_all)], 2)
+    return jnp.roll(g_now, (lax.axis_index("obs") + 1) * next_value.shape[2], 2)
 
 
 def from_behind(array, axis, by):
@@ -141,7 +155,7 @@
     def window_work(state_now, streams):
         beta_prior = state_now[:, :pred_count]
         info_prior = state_now[:, pred_count:]
-        all_coeffs = lax.all_gather(beta_prior, "obs", axis=2, tiled=True)
+        all_coeffs = drive_scales(beta_prior)
         channel = jnp.take(block_channel[0], streams, axis=0)
         block_coeffs = jax.vmap(lambda coeff_rows, chan: jnp.take(coeff_rows, chan, axis=1))(
             all_coeffs, channel

time: 692 us -> 729 us (1.053)
  waiting for transfers between devices: 30.8 us -> 205 us
  blocking collectives: 296 us -> 124 us
  starting transfers between devices: 145 us -> 168 us
  other arithmetic: 68.2 us -> 75.6 us
    ppermute x0 -> x49, waiting for transfers between devices: none -> 205 us  [drive_scales(): next_value = lax.ppermute(next_value, axis_name='obs', perm=met_up)]
    all_gather x7 -> x0, blocking collectives: 173 us -> none  [window_work(): all_coeffs = lax.all_gather(beta_prior, 'obs', axis=2, tiled=True)]
    all_to_all x7, waiting for transfers between devices: 30.8 us -> 0.02 us  [window_work(): lax.all_to_all(send_rows, 'obs', split_axis=1, concat_axis=1, tiled=True)]
    ppermute x0 -> x49, starting transfers between devices: none -> 13.1 us  [drive_scales(): next_value = lax.ppermute(next_value, axis_name='obs', perm=met_up)]
    all_to_all x7, starting transfers between devices: 26.2 us -> 37.1 us  [window_work(): lax.all_to_all(send_channel, 'obs', split_axis=1, concat_axis=1, tiled=True)]
  transfers between devices with their start and end apart: 21 -> 70, of which waited for: 7 -> 42; matrix products, arithmetic and copies ran while one was open for 18% -> 11% of each run, Pallas kernels for 0% -> 0%
where the time goes in v1:
time: 729 us; the launch traced here: 726 us
  waiting for transfers between devices  205 us (28%)
  starting transfers between devices  168 us (23%)
  blocking collectives  124 us (17%)
  local copies, waits for them, and re-layouts  112 us (15%)
  other arithmetic  75.6 us (10%)
  loops' own time  27.5 us (4%)
  matrix products  12.9 us (2%)
    ppermute x49, waiting for transfers between devices, drive_scales(): next_value = lax.ppermute(next_value, axis_name='obs', perm=met_up)  205 us
    psum x7, blocking collectives, window_work(): totals = lax.psum(statistics, 'obs')  124 us
    ppermute x7, starting transfers between devices, from_behind(): return lax.ppermute(array, axis, pairs)  94.1 us
    dynamic_update_slice x28, local copies, waits for them, and re-layouts, store_entry(): return lax.dynamic_update_slice_in_dim(buffer, updated, slot_index, 1)  43.8 us
    all_to_all x7, starting transfers between devices, window_work(): lax.all_to_all(send_channel, 'obs', split_axis=1, concat_axis=1, tiled=True)  37.1 us
    another operation x1, loops' own time, local(): lax.fori_loop(0, stream_count + section_count - 1, tick_step, initial)  27.5 us
    all_to_all x7, starting transfers between devices, window_work(): lax.all_to_all(send_rows, 'obs', split_axis=1, concat_axis=1, tiled=True)  23.5 us
  transfers between devices with their start and end apart: 70, of which 42 were waited for; matrix products, arithmetic and copies ran while one was open for 11% of the time, Pallas kernels for 0%

profile of v1, /device:TPU:1, one launch (start us, length us, event | category | flops | bytes accessed | tf_op | source)
XLA Modules:
  0.0 725.5 jit_solution(1649067539002671932)
XLA Ops:
  3.8 720.8 %while.38 = (s32[]{:T(128)}, f32[1,230,256]{2,1,0:T(8,128)S(1)}, f32[1,4,20,256]{3,1,2,0:T(4,128)S(1)}, f32[1,4,210,256]{3,1,2,0:T(4,128)S(1)}, s32[]{:T(128)}, ...) while((s32[]{:T(128)}, f32[1,230,256]{2,1,0:T(8,128)S(1)}, ...), condition=%wide.region_8.10_spmd.clone.clone, body=%wide.region_0.9_spmd.sunk.clone.clone.sunk | while | flops 57759528 | bytes 22234704 | solution.py:213
  24.0 5.4 collective-permute-done.2
  29.4 5.4 collective-permute-done.3
  40.1 5.4 collective-permute-done.5
  62.0 17.7 %psum.19 = f32[1,2]{1,0:T(1,128)S(1)} all-reduce(f32[1,2]{1,0:T(1,128)S(1)} %maximum_bitcast_fusion.6), channel_id=1, replica_groups=mesh['section'=4,'obs'=8] {'obs'}, use_global_device_ids=true, to_apply=%region_7.8 | all-reduce | flops 2 | bytes 16 | tf_op jit(solution)/shard_map/while/body/eval_jaxpr/psum | solution.py:170
  87.9 15.1 %collective-permute-start.7 = (f32[1,230,256]{2,1,0:T(8,128)S(1)}, f32[1,230,256]{2,1,0:T(8,128)S(1)}, u32[]{:S(2)}, u32[]{:S(2)}) collective-permute-start(f32[1,230,256]{2,1,0:T(8,128)S(1)} %pad_maximum_fusion.2), channel_id=1, source_target_pairs={{0,8},{8,16},{16,24},{1,9},{9,17},{17,25},{2,10},{10,18},{18,26},{... | collective-permute-start | bytes 706568 | tf_op jit(solution)/shard_map/while/body/eval_jaxpr/ppermute | solution.py:28
  103.4 5.9 dynamic_update_slice.31
  116.5 5.4 all-to-all-start.1
  128.3 5.4 collective-permute-done.2
  133.7 5.4 collective-permute-done.3
  144.5 5.3 collective-permute-done.5
  166.3 17.8 %psum.19 = f32[1,2]{1,0:T(1,128)S(1)} all-reduce(f32[1,2]{1,0:T(1,128)S(1)} %maximum_bitcast_fusion.6), channel_id=1, replica_groups=mesh['section'=4,'obs'=8] {'obs'}, use_global_device_ids=true, to_apply=%region_7.8 | all-reduce | flops 2 | bytes 16 | tf_op jit(solution)/shard_map/while/body/eval_jaxpr/psum | solution.py:170
  192.2 13.4 %collective-permute-start.7 = (f32[1,230,256]{2,1,0:T(8,128)S(1)}, f32[1,230,256]{2,1,0:T(8,128)S(1)}, u32[]{:S(2)}, u32[]{:S(2)}) collective-permute-start(f32[1,230,256]{2,1,0:T(8,128)S(1)} %pad_maximum_fusion.2), channel_id=1, source_target_pairs={{0,8},{8,16},{16,24},{1,9},{9,17},{17,25},{2,10},{10,18},{18,26},{... | collective-permute-start | bytes 706568 | tf_op jit(solution)/shard_map/while/body/eval_jaxpr/ppermute | solution.py:28
  205.9 5.9 dynamic_update_slice.31
  219.0 5.4 all-to-all-start.1
  230.9 5.6 collective-permute-done.2
  236.5 5.4 collective-permute-done.3
  247.3 5.3 collective-permute-done.5
  269.1 18.1 %psum.19 = f32[1,2]{1,0:T(1,128)S(1)} all-reduce(f32[1,2]{1,0:T(1,128)S(1)} %maximum_bitcast_fusion.6), channel_id=1, replica_groups=mesh['section'=4,'obs'=8] {'obs'}, use_global_device_ids=true, to_apply=%region_7.8 | all-reduce | flops 2 | bytes 16 | tf_op jit(solution)/shard_map/while/body/eval_jaxpr/psum | solution.py:170
  295.3 12.8 %collective-permute-start.7 = (f32[1,230,256]{2,1,0:T(8,128)S(1)}, f32[1,230,256]{2,1,0:T(8,128)S(1)}, u32[]{:S(2)}, u32[]{:S(2)}) collective-permute-start(f32[1,230,256]{2,1,0:T(8,128)S(1)} %pad_maximum_fusion.2), channel_id=1, source_target_pairs={{0,8},{8,16},{16,24},{1,9},{9,17},{17,25},{2,10},{10,18},{18,26},{... | collective-permute-start | bytes 706568 | tf_op jit(solution)/shard_map/while/body/eval_jaxpr/ppermute | solution.py:28
  308.5 5.9 dynamic_update_slice.31
  321.6 5.4 all-to-all-start.1
  333.4 5.4 collective-permute-done.2
  338.8 5.4 collective-permute-done.3
  349.6 5.3 collective-permute-done.5
  371.4 17.8 %psum.19 = f32[1,2]{1,0:T(1,128)S(1)} all-reduce(f32[1,2]{1,0:T(1,128)S(1)} %maximum_bitcast_fusion.6), channel_id=1, replica_groups=mesh['section'=4,'obs'=8] {'obs'}, use_global_device_ids=true, to_apply=%region_7.8 | all-reduce | flops 2 | bytes 16 | tf_op jit(solution)/shard_map/while/body/eval_jaxpr/psum | solution.py:170
  397.2 13.4 %collective-permute-start.7 = (f32[1,230,256]{2,1,0:T(8,128)S(1)}, f32[1,230,256]{2,1,0:T(8,128)S(1)}, u32[]{:S(2)}, u32[]{:S(2)}) collective-permute-start(f32[1,230,256]{2,1,0:T(8,128)S(1)} %pad_maximum_fusion.2), channel_id=1, source_target_pairs={{0,8},{8,16},{16,24},{1,9},{9,17},{17,25},{2,10},{10,18},{18,26},{... | collective-permute-start | bytes 706568 | tf_op jit(solution)/shard_map/while/body/eval_jaxpr/ppermute | solution.py:28
  411.0 5.9 dynamic_update_slice.31
  424.1 5.4 all-to-all-start.1
  436.0 5.4 collective-permute-done.2
  441.3 5.7 collective-permute-done.3
  474.2 17.7 %psum.19 = f32[1,2]{1,0:T(1,128)S(1)} all-reduce(f32[1,2]{1,0:T(1,128)S(1)} %maximum_bitcast_fusion.6), channel_id=1, replica_groups=mesh['section'=4,'obs'=8] {'obs'}, use_global_device_ids=true, to_apply=%region_7.8 | all-reduce | flops 2 | bytes 16 | tf_op jit(solution)/shard_map/while/body/eval_jaxpr/psum | solution.py:170
  500.1 13.1 %collective-permute-start.7 = (f32[1,230,256]{2,1,0:T(8,128)S(1)}, f32[1,230,256]{2,1,0:T(8,128)S(1)}, u32[]{:S(2)}, u32[]{:S(2)}) collective-permute-start(f32[1,230,256]{2,1,0:T(8,128)S(1)} %pad_maximum_fusion.2), channel_id=1, source_target_pairs={{0,8},{8,16},{16,24},{1,9},{9,17},{17,25},{2,10},{10,18},{18,26},{... | collective-permute-start | bytes 706568 | tf_op jit(solution)/shard_map/while/body/eval_jaxpr/ppermute | solution.py:28
  513.6 5.9 dynamic_update_slice.31
  526.7 5.4 all-to-all-start.1
  538.5 5.4 collective-permute-done.2
  543.9 5.4 collective-permute-done.3
  554.6 5.3 collective-permute-done.5
  576.5 17.7 %psum.19 = f32[1,2]{1,0:T(1,128)S(1)} all-reduce(f32[1,2]{1,0:T(1,128)S(1)} %maximum_bitcast_fusion.6), channel_id=1, replica_groups=mesh['section'=4,'obs'=8] {'obs'}, use_global_device_ids=true, to_apply=%region_7.8 | all-reduce | flops 2 | bytes 16 | tf_op jit(solution)/shard_map/while/body/eval_jaxpr/psum | solution.py:170
  602.3 13.4 %collective-permute-start.7 = (f32[1,230,256]{2,1,0:T(8,128)S(1)}, f32[1,230,256]{2,1,0:T(8,128)S(1)}, u32[]{:S(2)}, u32[]{:S(2)}) collective-permute-start(f32[1,230,256]{2,1,0:T(8,128)S(1)} %pad_maximum_fusion.2), channel_id=1, source_target_pairs={{0,8},{8,16},{16,24},{1,9},{9,17},{17,25},{2,10},{10,18},{18,26},{... | collective-permute-start | bytes 706568 | tf_op jit(solution)/shard_map/while/body/eval_jaxpr/ppermute | solution.py:28
  616.1 5.9 dynamic_update_slice.31
  629.2 5.4 all-to-all-start.1
  641.0 5.4 collective-permute-done.2
  646.4 5.4 collective-permute-done.3
  652.0 5.6 collective-permute-done.4
  679.5 17.7 %psum.19 = f32[1,2]{1,0:T(1,128)S(1)} all-reduce(f32[1,2]{1,0:T(1,128)S(1)} %maximum_bitcast_fusion.6), channel_id=1, replica_groups=mesh['section'=4,'obs'=8] {'obs'}, use_global_device_ids=true, to_apply=%region_7.8 | all-reduce | flops 2 | bytes 16 | tf_op jit(solution)/shard_map/while/body/eval_jaxpr/psum | solution.py:170
  705.3 13.0 %collective-permute-start.7 = (f32[1,230,256]{2,1,0:T(8,128)S(1)}, f32[1,230,256]{2,1,0:T(8,128)S(1)}, u32[]{:S(2)}, u32[]{:S(2)}) collective-permute-start(f32[1,230,256]{2,1,0:T(8,128)S(1)} %pad_maximum_fusion.2), channel_id=1, source_target_pairs={{0,8},{8,16},{16,24},{1,9},{9,17},{17,25},{2,10},{10,18},{18,26},{... | collective-permute-start | bytes 706568 | tf_op jit(solution)/shard_map/while/body/eval_jaxpr/ppermute | solution.py:28
  718.6 5.9 dynamic_update_slice.31
  (870 shorter events, 296.8 us)
Async XLA Ops:
  8.8 9.7 %collective-permute-start = (f32[1,20,256]{2,1,0:T(8,128)S(1)}, f32[1,20,256]{2,1,0:T(8,128)S(1)}, u32[]{:S(2)}, u32[]{:S(2)}) collective-permute-start(f32[1,20,256]{2,1,0:T(8,128)S(1)} %slice.5348), channel_id=1, source_target_pairs={{0,1},{1,2},{2,3},{3,4},{4,5},{5,6},{6,7},{7,0},{8,9},{9,10},{10,1... | collective-permute-start | bytes 61448 | tf_op jit(solution)/shard_map/while/body/eval_jaxpr/ppermute | solution.py:18
  13.0 32.8 %all-to-all-start.1 = ((f32[1,8,8]{2,0,1:T(1,128)}), f32[1,8,8]{2,0,1:T(1,128)S(1)}, u32[]{:S(2)}, u32[]{:S(2)}) async-start(f32[1,8,8]{2,0,1:T(1,128)} %bitcast.2454), calls=%async_computation.1 | async-start | bytes 8192 | tf_op jit(solution)/shard_map/while/body/eval_jaxpr/all_to_all | solution.py:174
  18.6 5.4 collective-permute-start.1
  24.0 5.4 collective-permute-start.2
  29.4 5.4 collective-permute-start.3
  40.1 5.5 collective-permute-start.5
  45.6 5.4 collective-permute-start.6
  58.7 23.0 %all-to-all-start = ((f32[1,8,8,230]{3,2,0,1:T(8,128)}), f32[1,8,8,230]{3,2,0,1:T(8,128)S(1)}, u32[]{:S(2)}, u32[]{:S(2)}) async-start(f32[1,8,8,230]{3,2,0,1:T(8,128)} %convolution_bitcast_fusion.4), calls=%async_computation | async-start | bytes 131072 | tf_op jit(solution)/shard_map/while/body/eval_jaxpr/all_to_all | solution.py:173
  87.9 21.4 %collective-permute-start.7 = (f32[1,230,256]{2,1,0:T(8,128)S(1)}, f32[1,230,256]{2,1,0:T(8,128)S(1)}, u32[]{:S(2)}, u32[]{:S(2)}) collective-permute-start(f32[1,230,256]{2,1,0:T(8,128)S(1)} %pad_maximum_fusion.2), channel_id=1, source_target_pairs={{0,8},{8,16},{16,24},{1,9},{9,17},{17,25},{2,10},{10,18},{18,26},{... | collective-permute-start | bytes 706568 | tf_op jit(solution)/shard_map/while/body/eval_jaxpr/ppermute | solution.py:28
  114.4 8.5 %collective-permute-start = (f32[1,20,256]{2,1,0:T(8,128)S(1)}, f32[1,20,256]{2,1,0:T(8,128)S(1)}, u32[]{:S(2)}, u32[]{:S(2)}) collective-permute-start(f32[1,20,256]{2,1,0:T(8,128)S(1)} %slice.5348), channel_id=1, source_target_pairs={{0,1},{1,2},{2,3},{3,4},{4,5},{5,6},{6,7},{7,0},{8,9},{9,10},{10,1... | collective-permute-start | bytes 61448 | tf_op jit(solution)/shard_map/while/body/eval_jaxpr/ppermute | solution.py:18
  116.5 33.5 %all-to-all-start.1 = ((f32[1,8,8]{2,0,1:T(1,128)}), f32[1,8,8]{2,0,1:T(1,128)S(1)}, u32[]{:S(2)}, u32[]{:S(2)}) async-start(f32[1,8,8]{2,0,1:T(1,128)} %bitcast.2454), calls=%async_computation.1 | async-start | bytes 8192 | tf_op jit(solution)/shard_map/while/body/eval_jaxpr/all_to_all | solution.py:174
  122.9 5.4 collective-permute-start.1
  144.4 5.4 collective-permute-start.5
  149.8 5.4 collective-permute-start.6
  162.9 23.0 %all-to-all-start = ((f32[1,8,8,230]{3,2,0,1:T(8,128)}), f32[1,8,8,230]{3,2,0,1:T(8,128)S(1)}, u32[]{:S(2)}, u32[]{:S(2)}) async-start(f32[1,8,8,230]{3,2,0,1:T(8,128)} %convolution_bitcast_fusion.4), calls=%async_computation | async-start | bytes 131072 | tf_op jit(solution)/shard_map/while/body/eval_jaxpr/all_to_all | solution.py:173
  192.2 19.7 %collective-permute-start.7 = (f32[1,230,256]{2,1,0:T(8,128)S(1)}, f32[1,230,256]{2,1,0:T(8,128)S(1)}, u32[]{:S(2)}, u32[]{:S(2)}) collective-permute-start(f32[1,230,256]{2,1,0:T(8,128)S(1)} %pad_maximum_fusion.2), channel_id=1, source_target_pairs={{0,8},{8,16},{16,24},{1,9},{9,17},{17,25},{2,10},{10,18},{18,26},{... | collective-permute-start | bytes 706568 | tf_op jit(solution)/shard_map/while/body/eval_jaxpr/ppermute | solution.py:28
  216.9 8.5 %collective-permute-start = (f32[1,20,256]{2,1,0:T(8,128)S(1)}, f32[1,20,256]{2,1,0:T(8,128)S(1)}, u32[]{:S(2)}, u32[]{:S(2)}) collective-permute-start(f32[1,20,256]{2,1,0:T(8,128)S(1)} %slice.5348), channel_id=1, source_target_pairs={{0,1},{1,2},{2,3},{3,4},{4,5},{5,6},{6,7},{7,0},{8,9},{9,10},{10,1... | collective-permute-start | bytes 61448 | tf_op jit(solution)/shard_map/while/body/eval_jaxpr/ppermute | solution.py:18
  219.0 33.8 %all-to-all-start.1 = ((f32[1,8,8]{2,0,1:T(1,128)}), f32[1,8,8]{2,0,1:T(1,128)S(1)}, u32[]{:S(2)}, u32[]{:S(2)}) async-start(f32[1,8,8]{2,0,1:T(1,128)} %bitcast.2454), calls=%async_computation.1 | async-start | bytes 8192 | tf_op jit(solution)/shard_map/while/body/eval_jaxpr/all_to_all | solution.py:174
  225.4 5.4 collective-permute-start.1
  230.9 5.6 collective-permute-start.2
  252.6 5.4 collective-permute-start.6
  265.7 23.3 %all-to-all-start = ((f32[1,8,8,230]{3,2,0,1:T(8,128)}), f32[1,8,8,230]{3,2,0,1:T(8,128)S(1)}, u32[]{:S(2)}, u32[]{:S(2)}) async-start(f32[1,8,8,230]{3,2,0,1:T(8,128)} %convolution_bitcast_fusion.4), calls=%async_computation | async-start | bytes 131072 | tf_op jit(solution)/shard_map/while/body/eval_jaxpr/all_to_all | solution.py:173
  295.3 19.1 %collective-permute-start.7 = (f32[1,230,256]{2,1,0:T(8,128)S(1)}, f32[1,230,256]{2,1,0:T(8,128)S(1)}, u32[]{:S(2)}, u32[]{:S(2)}) collective-permute-start(f32[1,230,256]{2,1,0:T(8,128)S(1)} %pad_maximum_fusion.2), channel_id=1, source_target_pairs={{0,8},{8,16},{16,24},{1,9},{9,17},{17,25},{2,10},{10,18},{18,26},{... | collective-permute-start | bytes 706568 | tf_op jit(solution)/shard_map/while/body/eval_jaxpr/ppermute | solution.py:28
  319.5 8.5 %collective-permute-start = (f32[1,20,256]{2,1,0:T(8,128)S(1)}, f32[1,20,256]{2,1,0:T(8,128)S(1)}, u32[]{:S(2)}, u32[]{:S(2)}) collective-permute-start(f32[1,20,256]{2,1,0:T(8,128)S(1)} %slice.5348), channel_id=1, source_target_pairs={{0,1},{1,2},{2,3},{3,4},{4,5},{5,6},{6,7},{7,0},{8,9},{9,10},{10,1... | collective-permute-start | bytes 61448 | tf_op jit(solution)/shard_map/while/body/eval_jaxpr/ppermute | solution.py:18
  321.6 33.5 %all-to-all-start.1 = ((f32[1,8,8]{2,0,1:T(1,128)}), f32[1,8,8]{2,0,1:T(1,128)S(1)}, u32[]{:S(2)}, u32[]{:S(2)}) async-start(f32[1,8,8]{2,0,1:T(1,128)} %bitcast.2454), calls=%async_computation.1 | async-start | bytes 8192 | tf_op jit(solution)/shard_map/while/body/eval_jaxpr/all_to_all | solution.py:174
  328.0 5.4 collective-permute-start.1
  344.2 5.4 collective-permute-start.4
  349.5 5.4 collective-permute-start.5
  354.9 5.4 collective-permute-start.6
  368.0 23.0 %all-to-all-start = ((f32[1,8,8,230]{3,2,0,1:T(8,128)}), f32[1,8,8,230]{3,2,0,1:T(8,128)S(1)}, u32[]{:S(2)}, u32[]{:S(2)}) async-start(f32[1,8,8,230]{3,2,0,1:T(8,128)} %convolution_bitcast_fusion.4), calls=%async_computation | async-start | bytes 131072 | tf_op jit(solution)/shard_map/while/body/eval_jaxpr/all_to_all | solution.py:173
  397.2 19.7 %collective-permute-start.7 = (f32[1,230,256]{2,1,0:T(8,128)S(1)}, f32[1,230,256]{2,1,0:T(8,128)S(1)}, u32[]{:S(2)}, u32[]{:S(2)}) collective-permute-start(f32[1,230,256]{2,1,0:T(8,128)S(1)} %pad_maximum_fusion.2), channel_id=1, source_target_pairs={{0,8},{8,16},{16,24},{1,9},{9,17},{17,25},{2,10},{10,18},{18,26},{... | collective-permute-start | bytes 706568 | tf_op jit(solution)/shard_map/while/body/eval_jaxpr/ppermute | solution.py:28
  422.0 8.5 %collective-permute-start = (f32[1,20,256]{2,1,0:T(8,128)S(1)}, f32[1,20,256]{2,1,0:T(8,128)S(1)}, u32[]{:S(2)}, u32[]{:S(2)}) collective-permute-start(f32[1,20,256]{2,1,0:T(8,128)S(1)} %slice.5348), channel_id=1, source_target_pairs={{0,1},{1,2},{2,3},{3,4},{4,5},{5,6},{6,7},{7,0},{8,9},{9,10},{10,1... | collective-permute-start | bytes 61448 | tf_op jit(solution)/shard_map/while/body/eval_jaxpr/ppermute | solution.py:18
  424.1 33.8 %all-to-all-start.1 = ((f32[1,8,8]{2,0,1:T(1,128)}), f32[1,8,8]{2,0,1:T(1,128)S(1)}, u32[]{:S(2)}, u32[]{:S(2)}) async-start(f32[1,8,8]{2,0,1:T(1,128)} %bitcast.2454), calls=%async_computation.1 | async-start | bytes 8192 | tf_op jit(solution)/shard_map/while/body/eval_jaxpr/all_to_all | solution.py:174
  430.5 5.4 collective-permute-start.1
  441.3 5.7 collective-permute-start.3
  470.9 23.0 %all-to-all-start = ((f32[1,8,8,230]{3,2,0,1:T(8,128)}), f32[1,8,8,230]{3,2,0,1:T(8,128)S(1)}, u32[]{:S(2)}, u32[]{:S(2)}) async-start(f32[1,8,8,230]{3,2,0,1:T(8,128)} %convolution_bitcast_fusion.4), calls=%async_computation | async-start | bytes 131072 | tf_op jit(solution)/shard_map/while/body/eval_jaxpr/all_to_all | solution.py:173
  500.1 19.4 %collective-permute-start.7 = (f32[1,230,256]{2,1,0:T(8,128)S(1)}, f32[1,230,256]{2,1,0:T(8,128)S(1)}, u32[]{:S(2)}, u32[]{:S(2)}) collective-permute-start(f32[1,230,256]{2,1,0:T(8,128)S(1)} %pad_maximum_fusion.2), channel_id=1, source_target_pairs={{0,8},{8,16},{16,24},{1,9},{9,17},{17,25},{2,10},{10,18},{18,26},{... | collective-permute-start | bytes 706568 | tf_op jit(solution)/shard_map/while/body/eval_jaxpr/ppermute | solution.py:28
  524.5 8.5 %collective-permute-start = (f32[1,20,256]{2,1,0:T(8,128)S(1)}, f32[1,20,256]{2,1,0:T(8,128)S(1)}, u32[]{:S(2)}, u32[]{:S(2)}) collective-permute-start(f32[1,20,256]{2,1,0:T(8,128)S(1)} %slice.5348), channel_id=1, source_target_pairs={{0,1},{1,2},{2,3},{3,4},{4,5},{5,6},{6,7},{7,0},{8,9},{9,10},{10,1... | collective-permute-start | bytes 61448 | tf_op jit(solution)/shard_map/while/body/eval_jaxpr/ppermute | solution.py:18
  526.7 33.5 %all-to-all-start.1 = ((f32[1,8,8]{2,0,1:T(1,128)}), f32[1,8,8]{2,0,1:T(1,128)S(1)}, u32[]{:S(2)}, u32[]{:S(2)}) async-start(f32[1,8,8]{2,0,1:T(1,128)} %bitcast.2454), calls=%async_computation.1 | async-start | bytes 8192 | tf_op jit(solution)/shard_map/while/body/eval_jaxpr/all_to_all | solution.py:174
  533.1 5.4 collective-permute-start.1
  573.1 23.0 %all-to-all-start = ((f32[1,8,8,230]{3,2,0,1:T(8,128)}), f32[1,8,8,230]{3,2,0,1:T(8,128)S(1)}, u32[]{:S(2)}, u32[]{:S(2)}) async-start(f32[1,8,8,230]{3,2,0,1:T(8,128)} %convolution_bitcast_fusion.4), calls=%async_computation | async-start | bytes 131072 | tf_op jit(solution)/shard_map/while/body/eval_jaxpr/all_to_all | solution.py:173
  602.3 19.7 %collective-permute-start.7 = (f32[1,230,256]{2,1,0:T(8,128)S(1)}, f32[1,230,256]{2,1,0:T(8,128)S(1)}, u32[]{:S(2)}, u32[]{:S(2)}) collective-permute-start(f32[1,230,256]{2,1,0:T(8,128)S(1)} %pad_maximum_fusion.2), channel_id=1, source_target_pairs={{0,8},{8,16},{16,24},{1,9},{9,17},{17,25},{2,10},{10,18},{18,26},{... | collective-permute-start | bytes 706568 | tf_op jit(solution)/shard_map/while/body/eval_jaxpr/ppermute | solution.py:28
  627.1 8.5 %collective-permute-start = (f32[1,20,256]{2,1,0:T(8,128)S(1)}, f32[1,20,256]{2,1,0:T(8,128)S(1)}, u32[]{:S(2)}, u32[]{:S(2)}) collective-permute-start(f32[1,20,256]{2,1,0:T(8,128)S(1)} %slice.5348), channel_id=1, source_target_pairs={{0,1},{1,2},{2,3},{3,4},{4,5},{5,6},{6,7},{7,0},{8,9},{9,10},{10,1... | collective-permute-start | bytes 61448 | tf_op jit(solution)/shard_map/while/body/eval_jaxpr/ppermute | solution.py:18
  629.2 34.0 %all-to-all-start.1 = ((f32[1,8,8]{2,0,1:T(1,128)}), f32[1,8,8]{2,0,1:T(1,128)S(1)}, u32[]{:S(2)}, u32[]{:S(2)}) async-start(f32[1,8,8]{2,0,1:T(1,128)} %bitcast.2454), calls=%async_computation.1 | async-start | bytes 8192 | tf_op jit(solution)/shard_map/while/body/eval_jaxpr/all_to_all | solution.py:174
  635.6 5.4 collective-permute-start.1
  651.8 5.8 collective-permute-start.4
  676.1 23.0 %all-to-all-start = ((f32[1,8,8,230]{3,2,0,1:T(8,128)}), f32[1,8,8,230]{3,2,0,1:T(8,128)S(1)}, u32[]{:S(2)}, u32[]{:S(2)}) async-start(f32[1,8,8,230]{3,2,0,1:T(8,128)} %convolution_bitcast_fusion.4), calls=%async_computation | async-start | bytes 131072 | tf_op jit(solution)/shard_map/while/body/eval_jaxpr/all_to_all | solution.py:173
  705.3 19.3 %collective-permute-start.7 = (f32[1,230,256]{2,1,0:T(8,128)S(1)}, f32[1,230,256]{2,1,0:T(8,128)S(1)}, u32[]{:S(2)}, u32[]{:S(2)}) collective-permute-start(f32[1,230,256]{2,1,0:T(8,128)S(1)} %pad_maximum_fusion.2), channel_id=1, source_target_pairs={{0,8},{8,16},{16,24},{1,9},{9,17},{17,25},{2,10},{10,18},{18,26},{... | collective-permute-start | bytes 706568 | tf_op jit(solution)/shard_map/while/body/eval_jaxpr/ppermute | solution.py:28
  (62 other events, 562.9 us)
